TPU v7x, 32 devices: a whole 2x2x4 slice. The times are simulated.
32 devices in a mesh: parts: 2 (over y), seq: 4 (over z), head: 4 (over x, core).
Axes of the slice: x: 2, y: 2, z: 4, core: 2. Of those that a mesh axis runs over, the one named last changes fastest.
Arguments:
- query_rows: bfloat16 [6144, 4096], P(('parts', 'seq', 'head')), parts along dimension 0, may hold values from -12 to 12
- key_rows: bfloat16 [6144, 4096], P(('parts', 'seq', 'head')), parts along dimension 0, may hold values from -12 to 12
- value_rows: bfloat16 [6144, 4096], P(('parts', 'seq', 'head')), parts along dimension 0, may hold values from -6 to 6
- block_lists: int32 [64, 4, 4, 3], P('parts', 'seq'), parts along dimension 0, may hold values from 0 to 5, as said below
- block_counts: int32 [64, 4, 4], P('parts'), parts along dimension 0, may hold values from 0 to 3, as said below
Outputs:
- attended: bfloat16 [6144, 4096], P(('parts', 'seq', 'head')), parts along dimension 0
There are 2 independent parts, one for each index of `parts`. A program takes and returns all parts, laid end to end along the dimension named above; each array names one. Nothing has to cross between parts.
Inputs may be any that keep to these rules, and one draw needn't show every extreme that they name: `block_lists`: for one head, query tile and key tile the 3 entries are distinct block numbers of the key tile; only the first block_counts of them are listed. `block_counts`: 0 where the key tile is the query tile; some entries of every draw equal 3; for every k, query tile and key tile, the counts of heads 2k and 2k+1 sum to at most 4, and exactly 4 for some k in every draw.
All inputs are finite; a program needn't handle non-finite values.
Results may differ from a plain program's by a relative error of at most 0.0034.
Values may be sent and summed in bfloat16 or wider, within the bound.
A program may use at most 64 MiB of HBM per device.

v0:
```python
import math

import jax
import jax.numpy as jnp
from jax import lax
from jax.sharding import PartitionSpec as P

HEADS = 32
DH = 128
BLOCK = 128
MOST = 3
PAIR_MOST = 4
TILE = 768


def score_block(head_queries, key_block, score_scale):
    products = lax.dot_general(
        head_queries, key_block, (((1,), (1,)), ((), ())), preferred_element_type=jnp.float32
    )
    return products * score_scale


def attend_head(head_queries, own_keys, own_values, flat_blocks, valid_slots, score_scale):
    scores = score_block(head_queries, own_keys, score_scale)
    run_max = jnp.max(scores, axis=1, keepdims=True)
    weights = jnp.exp(scores - run_max)
    run_sum = jnp.sum(weights, axis=1, keepdims=True)
    accum = jnp.dot(weights.astype(jnp.bfloat16), own_values, preferred_element_type=jnp.float32)
    group_size = max(1, 512 // BLOCK)
    slot_order = jnp.argsort(jnp.where(valid_slots, 0, 1), stable=True)
    used_count = jnp.sum(valid_slots.astype(jnp.int32))
    trip_count = (used_count + group_size - 1) // group_size

    def visit(turn_index, state_tuple):
        old_max, old_sum, old_accum = state_tuple
        picked = lax.dynamic_slice_in_dim(slot_order, turn_index * group_size, group_size)
        blocks = flat_blocks[picked].reshape(group_size * BLOCK, 2 * DH)
        live_keys = jnp.repeat(
            turn_index * group_size + jnp.arange(group_size, dtype=jnp.int32) < used_count, BLOCK
        )
        block_scores = score_block(head_queries, blocks[:, :DH], score_scale)
        block_scores = jnp.where(live_keys[None, :], block_scores, -jnp.inf)
        new_max = jnp.maximum(old_max, jnp.max(block_scores, axis=1, keepdims=True))
        block_weights = jnp.exp(block_scores - new_max)
        rescale = jnp.exp(old_max - new_max)
        new_sum = old_sum * rescale + jnp.sum(block_weights, axis=1, keepdims=True)
        new_accum = old_accum * rescale + jnp.dot(
            block_weights.astype(jnp.bfloat16), blocks[:, DH:], preferred_element_type=jnp.float32
        )
        return (new_max, new_sum, new_accum)

    run_max, run_sum, accum = lax.fori_loop(0, trip_count, visit, (run_max, run_sum, accum))
    return (accum / run_sum).astype(jnp.bfloat16)


def on_device(query_rows, key_rows, value_rows, block_lists, block_counts):
    head_count = lax.axis_size("head")
    seq_count = lax.axis_size("seq")
    seq_rank = lax.axis_index("seq")
    head_rank = lax.axis_index("head")
    local_heads = HEADS // head_count
    local_pairs = local_heads // 2
    score_scale = 1.0 / math.sqrt(DH)
    placed = jnp.arange(HEADS, dtype=jnp.int32)
    tile_queries, tile_keys, tile_values = (
        lax.all_to_all(query_rows, "head", split_axis=1, concat_axis=0, tiled=True),
        lax.all_to_all(key_rows, "head", split_axis=1, concat_axis=0, tiled=True),
        lax.all_to_all(value_rows, "head", split_axis=1, concat_axis=0, tiled=True),
    )
    my_heads = lax.dynamic_slice_in_dim(placed, head_rank * local_heads, local_heads)
    my_lists = block_lists[my_heads, 0]
    my_counts = jnp.take(block_counts[my_heads], seq_rank, axis=1)
    wanted = lax.all_to_all(
        jnp.transpose(my_lists, (1, 0, 2)), "seq", split_axis=0, concat_axis=0, tiled=True
    )
    block_total = TILE // BLOCK
    paired = jnp.concatenate(
        [
            tile_keys.reshape(block_total, BLOCK, local_heads, DH),
            tile_values.reshape(block_total, BLOCK, local_heads, DH),
        ],
        axis=3,
    )
    paired = jnp.transpose(paired, (2, 0, 1, 3))
    capacity_index = jnp.arange(PAIR_MOST, dtype=jnp.int32)
    asked_counts = jnp.take(block_counts[my_heads], seq_rank, axis=2)
    first_asked = jnp.transpose(asked_counts[0::2], (1, 0))[:, :, None]
    in_first = capacity_index[None, None, :] < first_asked
    slot_pick = jnp.clip(
        jnp.where(
            in_first, capacity_index[None, None, :], capacity_index[None, None, :] - first_asked
        ),
        0,
        MOST - 1,
    )
    head_pick = 2 * jnp.arange(local_pairs, dtype=jnp.int32)[None, :, None] + jnp.where(
        in_first, 0, 1
    )
    tile_pick = jnp.arange(seq_count, dtype=jnp.int32)[:, None, None]
    block_pick = wanted[tile_pick, head_pick, slot_pick]
    packed = paired[head_pick, block_pick]
    received = lax.all_to_all(packed, "seq", split_axis=0, concat_axis=0, tiled=True)
    outputs = []
    for head_slot in range(local_heads):
        head_queries = tile_queries[:, head_slot * DH : (head_slot + 1) * DH]
        own_keys = tile_keys[:, head_slot * DH : (head_slot + 1) * DH]
        own_values = tile_values[:, head_slot * DH : (head_slot + 1) * DH]
        pair_slot = head_slot // 2
        flat_blocks = received[:, pair_slot].reshape(seq_count * PAIR_MOST, BLOCK, 2 * DH)
        first_have = my_counts[2 * pair_slot][:, None]
        second_have = my_counts[2 * pair_slot + 1][:, None]
        if head_slot % 2 == 0:
            valid_grid = capacity_index[None, :] < first_have
        else:
            valid_grid = (capacity_index[None, :] >= first_have) & (
                capacity_index[None, :] < first_have + second_have
            )
        valid_slots = valid_grid.reshape(-1)
        outputs.append(
            attend_head(head_queries, own_keys, own_values, flat_blocks, valid_slots, score_scale)
        )
    tile_output = jnp.concatenate(outputs, axis=1)
    attended = lax.all_to_all(tile_output, "head", split_axis=0, concat_axis=1, tiled=True)
    return attended


def solution(mesh):
    in_specs = (
        P(("parts", "seq", "head"), None),
        P(("parts", "seq", "head"), None),
        P(("parts", "seq", "head"), None),
        P("parts", "seq", None, None),
        P("parts", None, None),
    )
    out_specs = P(("parts", "seq", "head"), None)
    return jax.shard_map(
        on_device, mesh=mesh, in_specs=in_specs, out_specs=out_specs, check_vma=False
    )
```

profile of v0, /device:TPU:0, one launch (start us, length us, event | category | flops | bytes accessed | tf_op | source)
XLA Modules:
  0.0 292.0 jit_solution(16236335125974565042)
XLA Ops:
  2.2 6.3 %all-to-all-start.3 = ((s32[4,8,3]{1,2,0:T(4,128)}), s32[4,8,3]{1,2,0:T(4,128)S(1)}, u32[]{:S(2)}, u32[]{:S(2)}) async-start(s32[4,8,3]{1,2,0:T(4,128)} %copy.49), calls=%async_computation.3 | async-start | bytes 16384 | tf_op jit(solution)/shard_map/all_to_all | solution.py:73
  8.5 2.7 copy.61
  11.2 2.9 all-to-all-done.3
  14.1 3.6 %all-to-all-start.1 = ((bf16[192,4,1024]{2,0,1:T(8,128)(2,1)}), bf16[192,4,1024]{2,0,1:T(8,128)(2,1)S(1)}, u32[]{:S(2)}, u32[]{:S(2)}) async-start(bf16[192,4,1024]{2,0,1:T(8,128)(2,1)} %bitcast.169), calls=%async_computation.1 | async-start | bytes 3145728 | tf_op jit(solution)/shard_map/all_to_all | solution.py:67
  17.7 2.7 copy.60
  20.4 17.3 %all-to-all-done.1 = bf16[192,4,1024]{2,0,1:T(8,128)(2,1)S(1)} async-done(((bf16[192,4,1024]{2,0,1:T(8,128)(2,1)}), bf16[192,4,1024]{2,0,1:T(8,128)(2,1)S(1)}, u32[]{:S(2)}, u32[]{:S(2)}) %all-to-all-start.1) | async-done | bytes 1572896 | tf_op jit(solution)/shard_map/all_to_all | solution.py:67
  38.8 3.6 %all-to-all-start.2 = ((bf16[192,4,1024]{2,0,1:T(8,128)(2,1)}), bf16[192,4,1024]{2,0,1:T(8,128)(2,1)S(1)}, u32[]{:S(2)}, u32[]{:S(2)}) async-start(bf16[192,4,1024]{2,0,1:T(8,128)(2,1)} %bitcast.168), calls=%async_computation.2 | async-start | bytes 3145728 | tf_op jit(solution)/shard_map/all_to_all | solution.py:68
  43.2 2.7 copy.62
  46.3 16.2 %all-to-all-done.2 = bf16[192,4,1024]{2,0,1:T(8,128)(2,1)S(1)} async-done(((bf16[192,4,1024]{2,0,1:T(8,128)(2,1)}), bf16[192,4,1024]{2,0,1:T(8,128)(2,1)S(1)}, u32[]{:S(2)}, u32[]{:S(2)}) %all-to-all-start.2) | async-done | bytes 1572896 | tf_op jit(solution)/shard_map/all_to_all | solution.py:68
  62.4 4.3 %all-to-all-start = ((bf16[192,4,1024]{2,0,1:T(8,128)(2,1)}), bf16[192,4,1024]{2,0,1:T(8,128)(2,1)}, u32[]{:S(2)}, u32[]{:S(2)}) async-start(bf16[192,4,1024]{2,0,1:T(8,128)(2,1)} %bitcast.167), calls=%async_computation | async-start | bytes 3145728 | tf_op jit(solution)/shard_map/all_to_all | solution.py:66
  74.7 1.3 sort.122
  76.0 1.3 sort.121
  78.6 1.3 sort.119
  81.2 1.3 sort.117
  82.5 1.3 sort.116
  86.4 1.8 copy.55
  89.9 2.8 gather_fusion.11
  92.7 5.0 %all-to-all-start.4 = ((bf16[4,4,4,128,256]{4,3,2,1,0:T(8,128)(2,1)}), bf16[4,4,4,128,256]{4,3,2,1,0:T(8,128)(2,1)}, u32[]{:S(2)}, u32[]{:S(2)}) async-start(bf16[4,4,4,128,256]{4,3,2,1,0:T(8,128)(2,1)} %bitcast.144), calls=%async_computation.4 | async-start | bytes 8388608 | tf_op jit(solution)/shard_map/all_to_all | solution.py:102
  97.8 1.5 multiply_reduce_fusion
  99.7 1.5 multiply_reduce_fusion.1
  101.7 1.5 multiply_reduce_fusion.2
  103.6 1.5 multiply_reduce_fusion.3
  105.6 1.5 multiply_reduce_fusion.4
  107.5 1.5 multiply_reduce_fusion.5
  109.5 1.5 multiply_reduce_fusion.6
  111.4 1.5 multiply_reduce_fusion.7
  113.4 2.8 fusion.176
  120.7 71.0 %all-to-all-done.4 = bf16[4,4,4,128,256]{4,3,2,1,0:T(8,128)(2,1)} async-done(((bf16[4,4,4,128,256]{4,3,2,1,0:T(8,128)(2,1)}), bf16[4,4,4,128,256]{4,3,2,1,0:T(8,128)(2,1)}, u32[]{:S(2)}, u32[]{:S(2)}) %all-to-all-start.4) | async-done | bytes 4194336 | tf_op jit(solution)/shard_map/all_to_all | solution.py:102
  191.7 4.3 %fusion.175 = (bf16[4,1,4,128,256]{4,3,2,1,0:T(8,128)(2,1)}, bf16[4,1,4,128,256]{4,3,2,1,0:T(8,128)(2,1)}, bf16[4,1,4,128,256]{4,3,2,1,0:T(8,128)(2,1)}, bf16[4,1,4,128,256]{4,3,2,1,0:T(8,128)(2,1)}) fusion(bf16[4,4,4,128,256]{4,3,2,1,0:T(8,128)(2,1)} %all-to-all-done.4), kind=kLoop, calls=%fused_computation.321 | loop fusion | bytes 8388608 | tf_op jit(solution)/shard_map/slice | solution.py:109
  196.1 4.8 %while.118 = (s32[]{:T(128)}, f32[768,1]{0,1:T(1,128)S(1)}, f32[768,1]{0,1:T(1,128)S(1)}, f32[768,128]{1,0:T(8,128)S(1)}, s32[]{:T(128)}, /*index=5*/s32[]{:T(12...) while((s32[]{:T(128)}, f32[768,1]{0,1:T(1,128)S(1)}, ...), condition=%wide.region_39.40_spmd, body=%wide.region_36.39_spmd.sunk | while | flops 204279072 | bytes 6547711 | solution.py:52
  196.2 1.8 gather_fusion.4
  200.9 4.8 %while.117 = (s32[]{:T(128)}, f32[768,1]{0,1:T(1,128)S(1)}, f32[768,1]{0,1:T(1,128)S(1)}, f32[768,128]{1,0:T(8,128)S(1)}, s32[]{:T(128)}, /*index=5*/s32[]{:T(12...) while((s32[]{:T(128)}, f32[768,1]{0,1:T(1,128)S(1)}, ...), condition=%wide.region_31.32_spmd, body=%wide.region_28.31_spmd.sunk | while | flops 204279072 | bytes 6547711 | solution.py:52
  201.0 1.8 gather_fusion.3
  205.8 9.7 %while.116 = (s32[]{:T(128)}, f32[768,1]{0,1:T(1,128)S(1)}, f32[768,1]{0,1:T(1,128)S(1)}, f32[768,128]{1,0:T(8,128)S(1)}, s32[]{:T(128)}, /*index=5*/s32[]{:T(12...) while((s32[]{:T(128)}, f32[768,1]{0,1:T(1,128)S(1)}, ...), condition=%wide.region_23.24_spmd, body=%wide.region_20.23_spmd.sunk | while | flops 204279072 | bytes 6547711 | solution.py:52
  205.9 1.8 gather_fusion.2
  208.4 1.3 fusion.248
  210.7 1.8 gather_fusion.2
  213.3 1.3 fusion.248
  215.5 4.8 %while.115 = (s32[]{:T(128)}, f32[768,1]{0,1:T(1,128)S(1)}, f32[768,1]{0,1:T(1,128)S(1)}, f32[768,128]{1,0:T(8,128)S(1)}, s32[]{:T(128)}, /*index=5*/s32[]{:T(12...) while((s32[]{:T(128)}, f32[768,1]{0,1:T(1,128)S(1)}, ...), condition=%wide.region_15.16_spmd, body=%wide.region_12.15_spmd.sunk | while | flops 204279072 | bytes 6547711 | solution.py:52
  215.6 1.8 gather_fusion.1
  220.3 14.3 %while.114 = (s32[]{:T(128)}, f32[768,1]{0,1:T(1,128)S(1)}, f32[768,1]{0,1:T(1,128)S(1)}, f32[768,128]{1,0:T(8,128)S(1)}, s32[]{:T(128)}, /*index=5*/s32[]{:T(12...) while((s32[]{:T(128)}, f32[768,1]{0,1:T(1,128)S(1)}, ...), condition=%wide.region_7.8_spmd, body=%wide.region_4.7_spmd.sunk | while | flops 204279072 | bytes 6547711 | solution.py:52
  220.4 1.8 gather_fusion
  222.9 1.3 fusion.236
  225.2 1.8 gather_fusion
  227.7 1.3 fusion.236
  230.0 1.8 gather_fusion
  236.4 54.3 %all_to_all.86 = bf16[4,192,1024]{2,1,0:T(8,128)(2,1)S(1)} all-to-all(bf16[4,192,1024]{2,1,0:T(8,128)(2,1)S(1)} %bitcast.173), channel_id=1, replica_groups=mesh['parts'=2,'seq'=4,'head'=4] {'head'}, dimensions={0} | all-to-all | bytes 3145728 | tf_op jit(solution)/shard_map/all_to_all | solution.py:123
  290.7 1.3 copy.54
  (186 shorter events, 42.1 us)
Async XLA Ops:
  2.2 11.9 %all-to-all-start.3 = ((s32[4,8,3]{1,2,0:T(4,128)}), s32[4,8,3]{1,2,0:T(4,128)S(1)}, u32[]{:S(2)}, u32[]{:S(2)}) async-start(s32[4,8,3]{1,2,0:T(4,128)} %copy.49), calls=%async_computation.3 | async-start | bytes 16384 | tf_op jit(solution)/shard_map/all_to_all | solution.py:73
  14.1 23.6 %all-to-all-start.1 = ((bf16[192,4,1024]{2,0,1:T(8,128)(2,1)}), bf16[192,4,1024]{2,0,1:T(8,128)(2,1)S(1)}, u32[]{:S(2)}, u32[]{:S(2)}) async-start(bf16[192,4,1024]{2,0,1:T(8,128)(2,1)} %bitcast.169), calls=%async_computation.1 | async-start | bytes 3145728 | tf_op jit(solution)/shard_map/all_to_all | solution.py:67
  37.7 1.1 copy-start.2
  37.7 4.7 %copy-start.3 = (s32[32,4,4]{0,2,1:T(4,128)S(1)}, s32[32,4,4]{0,2,1:T(4,128)}, u32[]{:S(2)}) copy-start(s32[32,4,4]{0,2,1:T(4,128)} %param.25) | copy-start | bytes 6148
  38.8 23.6 %all-to-all-start.2 = ((bf16[192,4,1024]{2,0,1:T(8,128)(2,1)}), bf16[192,4,1024]{2,0,1:T(8,128)(2,1)S(1)}, u32[]{:S(2)}, u32[]{:S(2)}) async-start(bf16[192,4,1024]{2,0,1:T(8,128)(2,1)} %bitcast.168), calls=%async_computation.2 | async-start | bytes 3145728 | tf_op jit(solution)/shard_map/all_to_all | solution.py:68
  62.4 26.2 %copy-start = (bf16[192,4,1024]{2,0,1:T(8,128)(2,1)}, bf16[192,4,1024]{2,0,1:T(8,128)(2,1)S(1)}, u32[]{:S(2)}) copy-start(bf16[192,4,1024]{2,0,1:T(8,128)(2,1)S(1)} %all-to-all-done.2) | copy-start | bytes 4718596
  62.4 30.3 %all-to-all-start = ((bf16[192,4,1024]{2,0,1:T(8,128)(2,1)}), bf16[192,4,1024]{2,0,1:T(8,128)(2,1)}, u32[]{:S(2)}, u32[]{:S(2)}) async-start(bf16[192,4,1024]{2,0,1:T(8,128)(2,1)} %bitcast.167), calls=%async_computation | async-start | bytes 3145728 | tf_op jit(solution)/shard_map/all_to_all | solution.py:66
  92.7 99.0 %all-to-all-start.4 = ((bf16[4,4,4,128,256]{4,3,2,1,0:T(8,128)(2,1)}), bf16[4,4,4,128,256]{4,3,2,1,0:T(8,128)(2,1)}, u32[]{:S(2)}, u32[]{:S(2)}) async-start(bf16[4,4,4,128,256]{4,3,2,1,0:T(8,128)(2,1)} %bitcast.144), calls=%async_computation.4 | async-start | bytes 8388608 | tf_op jit(solution)/shard_map/all_to_all | solution.py:102
  113.4 2.8 copy-start.1
where the time goes:
time: 292 us
  waiting for transfers between devices  107 us (37%)
  blocking collectives  54.3 us (19%)
  local copies, waits for them, and re-layouts  43.7 us (15%)
  matrix products  31.2 us (11%)
  other arithmetic  26.3 us (9%)
  starting transfers between devices  22.9 us (8%)
  between operations  5.64 us (2%)
    all_to_all x1, waiting for transfers between devices, on_device(): lax.all_to_all(packed, 'seq', split_axis=0, concat_axis=0, tiled=True)  71 us
    all_to_all x1, blocking collectives, on_device(): lax.all_to_all(tile_output, 'head', split_axis=0, concat_axis=1, tiled=True)  54.3 us
    dot_general x16, matrix products, score_block(): lax.dot_general(head_queries, key_block, (((1,), (1,)), ((), ())), prefer...  22.5 us
    all_to_all x1, waiting for transfers between devices, on_device(): lax.all_to_all(key_rows, 'head', split_axis=1, concat_axis=0, tiled=True)  17.3 us
    all_to_all x1, waiting for transfers between devices, on_device(): lax.all_to_all(value_rows, 'head', split_axis=1, concat_axis=0, tiled=True)  16.2 us
    gather x8, local copies, waits for them, and re-layouts, visit(): blocks = flat_blocks[picked].reshape(group_size * BLOCK, 2 * DH)  14.3 us
    sort x8, other arithmetic, attend_head(): slot_order = jnp.argsort(jnp.where(valid_slots, 0, 1), stable=True)  10.4 us
    all_to_all x1, starting transfers between devices, on_device(): lax.all_to_all(jnp.transpose(my_lists, (1, 0, 2)), 'seq', split_axis=0, c...  6.35 us
  transfers between devices with their start and end apart: 5, of which 4 were waited for; matrix products, arithmetic and copies ran while one was open for 18% of the time, Pallas kernels for 0%

commit v1 on v0

v1 whole, which is shorter than its diff:
```python
import functools
import math

import jax
import jax.numpy as jnp
from jax import lax
from jax.experimental import pallas as pl
from jax.experimental.pallas import tpu as pltpu
from jax.sharding import PartitionSpec as P

HEADS = 32
DH = 128
BLOCK = 128
MOST = 3
PAIR_MOST = 4
TILE = 768
MESH = pl.DeviceIdType.MESH


def contract_last(a, b):
    return lax.dot_general(a, b, (((1,), (1,)), ((), ())), preferred_element_type=jnp.float32)


def body(dims, lists_ref, counts_ref, q_ref, k_ref, v_ref, out_ref, *scratch):
    H, S, rows, heads, piece = dims
    pairs = heads // 2
    chips = H // 2
    kb, vb, qb = scratch[:pairs], scratch[pairs : 2 * pairs], scratch[2 * pairs : 3 * pairs]
    (ob, pk, fk, lbuf, lsm, x_send, x_recv, z_send, z_recv, l_send, l_recv, l_loc, o_send, o_recv) = (
        scratch[3 * pairs :]
    )
    me = lax.axis_index("head")
    tile = lax.axis_index("seq")

    def peer_of(i):
        chip = lax.rem(lax.div(me, 2) + 1 + lax.div(i, 2), chips)
        return chip * 2 + lax.rem(me + i + 1, 2)

    def source_of(i):
        chip = lax.rem(lax.div(me, 2) + 2 * chips - 1 - lax.div(i, 2), chips)
        return chip * 2 + lax.rem(me + i + 1, 2)

    def tile_after(d):
        return lax.rem(tile + d, S)

    def i32(i):
        return jnp.int32(i)

    barrier = pltpu.get_barrier_semaphore()
    for i in range(H - 1):
        pl.semaphore_signal(barrier, inc=1, device_id={"head": peer_of(i32(i))}, device_id_type=MESH)
    for d in range(1, S):
        pl.semaphore_signal(barrier, inc=1, device_id={"seq": tile_after(d)}, device_id_type=MESH)

    sources = (k_ref, v_ref, q_ref)
    places = (kb, vb, qb)

    def pair_columns(owner, p):
        return pl.ds(pl.multiple_of((owner * heads + 2 * p) * DH, 2 * DH), 2 * DH)

    def row_range(owner):
        return pl.ds(pl.multiple_of(owner * rows, 16), rows)

    def source_at(a, owner, p):
        columns = pair_columns(owner, p)
        return sources[a].at[:, columns] if a == 2 else sources[a].at[:, :, columns]

    def place_at(a, owner, p):
        if a == 2:
            return places[a][p].at[row_range(owner), :]
        return places[a][p].at[pl.ds(owner * (rows // piece), rows // piece)]

    def own_copy(a, p):
        return pltpu.make_async_copy(
            source_at(a, me, p),
            place_at(a, me, p),
            x_recv.at[a, p, H - 1],
        )

    def x_copy(a, p, i, landed):
        to = peer_of(i32(i))
        at = source_of(i32(i)) if landed else me
        return pltpu.make_async_remote_copy(
            src_ref=source_at(a, to, p),
            dst_ref=place_at(a, at, p),
            send_sem=x_send.at[a, p, i],
            recv_sem=x_recv.at[a, p, i],
            device_id={"head": to},
            device_id_type=MESH,
        )

    def l_copy(d):
        to = tile_after(d)
        return pltpu.make_async_remote_copy(
            src_ref=lists_ref.at[to],
            dst_ref=lbuf.at[d - 1],
            send_sem=l_send.at[d - 1],
            recv_sem=l_recv.at[d - 1],
            device_id={"seq": to},
            device_id_type=MESH,
        )

    def z_copy(p, d):
        return pltpu.make_async_remote_copy(
            src_ref=pk.at[p, d - 1],
            dst_ref=fk.at[p, d - 1],
            send_sem=z_send.at[p, d - 1],
            recv_sem=z_recv.at[p, d - 1],
            device_id={"seq": tile_after(d)},
            device_id_type=MESH,
        )

    def o_copy(p, i, landed):
        to = peer_of(i)
        at = source_of(i) if landed else me
        return pltpu.make_async_remote_copy(
            src_ref=ob.at[p, i],
            dst_ref=out_ref.at[:, pair_columns(at, p)],
            send_sem=o_send.at[p, i],
            recv_sem=o_recv.at[p, i],
            device_id={"head": to},
            device_id_type=MESH,
        )

    def o_own(p):
        return pltpu.make_async_copy(
            ob.at[p, H - 1], out_ref.at[:, pair_columns(me, p)], o_recv.at[p, H - 1]
        )

    for p in range(pairs):
        for a in (0, 1):
            own_copy(a, p).start()
    for p in range(pairs):
        own_copy(2, p).start()
    pl.semaphore_wait(barrier, H - 1 + S - 1)
    for d in range(1, S):
        l_copy(d).start()
    for p in range(pairs):
        for a in (0, 1):
            for i in range(H - 1):
                x_copy(a, p, i, False).start()
    for p in range(pairs):
        for i in range(H - 1):
            x_copy(2, p, i, False).start()

    for d in range(1, S):
        l_copy(d).wait_recv()
    to_scalars = pltpu.make_async_copy(lbuf, lsm, l_loc)
    to_scalars.start()
    to_scalars.wait()

    def arrived(a, p):
        own_copy(a, p).wait()
        for i in range(H - 1):
            x_copy(a, p, i, True).wait_recv()

    def count_of(head_slot, query_tile, key_tile):
        return counts_ref[((me * heads + head_slot) * S + query_tile) * S + key_tile]

    for p in range(pairs):
        arrived(0, p)
        arrived(1, p)
        for d in range(1, S):
            first = count_of(2 * p, tile_after(d), tile)
            for s in range(PAIR_MOST):
                left = lsm[S - d - 1, 0, 2 * p * MOST + min(s, MOST - 1)]
                right = lsm[S - d - 1, 0, (2 * p + 1) * MOST + min(PAIR_MOST - 1 - s, MOST - 1)]
                for b in range(BLOCK // piece):
                    at = pl.ds(b * piece, piece)
                    for c, held in enumerate((kb[p], vb[p])):
                        if s < PAIR_MOST - 1:
                            chosen = held[left * (BLOCK // piece) + b, :, :DH]
                        if s > 0:
                            other = held[right * (BLOCK // piece) + b, :, DH:]
                            if s < PAIR_MOST - 1:
                                chosen = jnp.where(s < first, chosen, other)
                            else:
                                chosen = other
                        pk[p, d - 1, c, s, at, :] = chosen
            z_copy(p, d).start()

    factor = math.log2(math.e) / math.sqrt(DH)
    width = MOST * BLOCK
    lane = lax.broadcasted_iota(jnp.int32, (1, width), 1)
    for p in range(pairs):
        arrived(2, p)
        for d in range(1, S):
            z_copy(p, d).wait_recv()

        def chunk(i, carry, p=p):
            mine = row_range(peer_of(i))
            for hs in range(2):
                cols = slice(hs * DH, (hs + 1) * DH)
                q = qb[p][mine, cols]
                scores = [contract_last(q, kb[p][:, :, cols].reshape(TILE, DH))]
                values = [vb[p][:, :, cols].reshape(TILE, DH)]
                for d in range(1, S):
                    used = count_of(2 * p + hs, tile, lax.rem(tile + S - d, S)) * BLOCK
                    live = lane < used if hs == 0 else lane >= width - used
                    bias = jnp.where(live, 0.0, -jnp.inf).astype(jnp.float32)
                    far = fk[p, d - 1, 0, hs : hs + MOST].reshape(width, DH)
                    scores.append(contract_last(q, far) + bias)
                    values.append(fk[p, d - 1, 1, hs : hs + MOST].reshape(width, DH))
                top = functools.reduce(
                    jnp.maximum, [jnp.max(s, axis=1, keepdims=True) for s in scores]
                )
                total = jnp.zeros((rows, 1), jnp.float32)
                mixed = jnp.zeros((rows, DH), jnp.float32)
                for s, v in zip(scores, values):
                    w = jnp.exp2((s - top) * factor)
                    total = total + jnp.sum(w, axis=1, keepdims=True)
                    mixed = mixed + jnp.dot(
                        w.astype(jnp.bfloat16), v, preferred_element_type=jnp.float32
                    )
                ob[p, i, :, cols] = (mixed / total).astype(jnp.bfloat16)

            @pl.when(i < H - 1)
            def _():
                o_copy(p, i, False).start()

            return carry

        lax.fori_loop(0, H, chunk, 0)
        o_own(p).start()

    for p in range(pairs):
        o_own(p).wait()
        for i in range(H - 1):
            o_copy(p, i32(i), True).wait_recv()
    for d in range(1, S):
        l_copy(d).wait_send()
        for p in range(pairs):
            z_copy(p, d).wait_send()
    for p in range(pairs):
        for i in range(H - 1):
            for a in range(3):
                x_copy(a, p, i, False).wait_send()
            o_copy(p, i32(i), False).wait_send()


def on_device(query_rows, key_rows, value_rows, block_lists, block_counts):
    H = lax.axis_size("head")
    S = lax.axis_size("seq")
    me = lax.axis_index("head")
    rows = query_rows.shape[0]
    heads = HEADS // H
    pairs = heads // 2
    mine = lax.dynamic_slice_in_dim(block_lists[:, 0], me * heads, heads)
    lists = jnp.transpose(mine, (1, 0, 2)).reshape(S, 1, heads * MOST)
    lists = jnp.pad(lists, ((0, 0), (0, 0), (0, 128 - heads * MOST)))
    bf16 = jnp.bfloat16
    piece = math.gcd(rows, BLOCK)
    pieces = (rows // piece, piece, query_rows.shape[1])
    tile_buffers = [
        pltpu.VMEM((TILE // piece, piece, 2 * DH), bf16) for _ in range(2 * pairs)
    ] + [pltpu.VMEM((TILE, 2 * DH), bf16) for _ in range(pairs)]
    anywhere = pl.BlockSpec(memory_space=pl.ANY)
    return pl.pallas_call(
        functools.partial(body, (H, S, rows, heads, piece)),
        out_shape=jax.ShapeDtypeStruct(query_rows.shape, bf16),
        in_specs=[anywhere, pl.BlockSpec(memory_space=pltpu.SMEM), anywhere, anywhere, anywhere],
        out_specs=anywhere,
        scratch_shapes=tile_buffers
        + [
            pltpu.VMEM((pairs, H, rows, 2 * DH), bf16),
            pltpu.VMEM((pairs, S - 1, 2, PAIR_MOST, BLOCK, DH), bf16),
            pltpu.VMEM((pairs, S - 1, 2, PAIR_MOST, BLOCK, DH), bf16),
            pltpu.VMEM((S - 1, 1, 128), jnp.int32),
            pltpu.SMEM((S - 1, 1, 128), jnp.int32),
            pltpu.SemaphoreType.DMA((3, pairs, H)),
            pltpu.SemaphoreType.DMA((3, pairs, H)),
            pltpu.SemaphoreType.DMA((pairs, S - 1)),
            pltpu.SemaphoreType.DMA((pairs, S - 1)),
            pltpu.SemaphoreType.DMA((S - 1,)),
            pltpu.SemaphoreType.DMA((S - 1,)),
            pltpu.SemaphoreType.DMA,
            pltpu.SemaphoreType.DMA((pairs, H)),
            pltpu.SemaphoreType.DMA((pairs, H)),
        ],
        compiler_params=pltpu.CompilerParams(
            collective_id=0, has_side_effects=True, vmem_limit_bytes=60 << 20
        ),
        name="block_attention",
    )(lists, block_counts.reshape(-1), query_rows, key_rows.reshape(pieces), value_rows.reshape(pieces))


def solution(mesh):
    in_specs = (
        P(("parts", "seq", "head"), None),
        P(("parts", "seq", "head"), None),
        P(("parts", "seq", "head"), None),
        P("parts", "seq", None, None),
        P("parts", None, None),
    )
    out_specs = P(("parts", "seq", "head"), None)
    return jax.shard_map(
        on_device, mesh=mesh, in_specs=in_specs, out_specs=out_specs, check_vma=False
    )
```

time: 292 us -> 119 us (0.41)
  the two profiles are of different devices: /device:TPU:0 before, /device:TPU:8 now
where the time goes in v1:
time: 119 us
  Pallas kernels  113 us (95%)
  local copies, waits for them, and re-layouts  5.75 us (5%)
    pallas_call x1, Pallas kernels, on_device(): pl.pallas_call(functools.partial(body, (H, S, rows, heads, piece)), out_s...  113 us
    unnamed x4, local copies, waits for them, and re-layouts  4.2 us

profile of v1, /device:TPU:8, one launch (start us, length us, event | category | flops | bytes accessed | tf_op | source)
XLA Modules:
  0.0 119.1 jit_solution(5975548873979613335)
XLA Ops:
  0.0 0.0 copy-start
  0.0 0.7 copy-done
  0.7 0.1 dynamic-slice_bitcast_fusion
  0.8 0.1 copy.8
  0.9 0.1 reshape.13
  0.9 0.6 pad.4.lists_ref
  1.5 0.8 copy.10
  2.3 0.7 reshape.14.counts_ref
  3.0 113.3 %block_attention.1 = bf16[192,4096]{1,0:T(8,128)(2,1)} custom-call(s32[4,1,128]{2,1,0:T(1,128)} %pad.4.lists_ref, s32[512]{0:T(512)} %reshape.14.counts_ref, bf16[192,4096]{1,0:T(8,128)(2,1)} %q_ref.1, bf16[3,64,4096]{2,1,0:T(8,128)(2,1)} %bitcast.7, bf16[3,64,4096]{2,1,0:T(8,128)(2,1)} %bitcast.8), custom_call_target="tpu_custom_call" | custom-call | tf_op jit(solution)/shard_map/block_attention/pallas_call | solution.py:258
  116.4 2.7 %copy.12 = bf16[192,4096]{1,0:T(8,128)(2,1)} copy(bf16[192,4096]{1,0:T(8,128)(2,1)} %block_attention.1) | data formatting | bytes 3145728
Async XLA Ops:
  0.0 0.7 copy-start

commit v2 on v1

--- a/solution.py
+++ b/solution.py
@@ -100,12 +100,12 @@
             device_id_type=MESH,
         )
 
-    def z_copy(p, d):
-        return pltpu.make_async_remote_copy(
-            src_ref=pk.at[p, d - 1],
-            dst_ref=fk.at[p, d - 1],
-            send_sem=z_send.at[p, d - 1],
-            recv_sem=z_recv.at[p, d - 1],
+    def z_copy(p, d, c):
+        return pltpu.make_async_remote_copy(
+            src_ref=pk.at[p, d - 1, c],
+            dst_ref=fk.at[p, d - 1, c],
+            send_sem=z_send.at[p, d - 1, c],
+            recv_sem=z_recv.at[p, d - 1, c],
             device_id={"seq": tile_after(d)},
             device_id_type=MESH,
         )
@@ -127,11 +127,6 @@
             ob.at[p, H - 1], out_ref.at[:, pair_columns(me, p)], o_recv.at[p, H - 1]
         )
 
-    for p in range(pairs):
-        for a in (0, 1):
-            own_copy(a, p).start()
-    for p in range(pairs):
-        own_copy(2, p).start()
     pl.semaphore_wait(barrier, H - 1 + S - 1)
     for d in range(1, S):
         l_copy(d).start()
@@ -139,9 +134,11 @@
         for a in (0, 1):
             for i in range(H - 1):
                 x_copy(a, p, i, False).start()
+            own_copy(a, p).start()
     for p in range(pairs):
         for i in range(H - 1):
             x_copy(2, p, i, False).start()
+        own_copy(2, p).start()
 
     for d in range(1, S):
         l_copy(d).wait_recv()
@@ -158,16 +155,14 @@
         return counts_ref[((me * heads + head_slot) * S + query_tile) * S + key_tile]
 
     for p in range(pairs):
-        arrived(0, p)
-        arrived(1, p)
-        for d in range(1, S):
-            first = count_of(2 * p, tile_after(d), tile)
-            for s in range(PAIR_MOST):
-                left = lsm[S - d - 1, 0, 2 * p * MOST + min(s, MOST - 1)]
-                right = lsm[S - d - 1, 0, (2 * p + 1) * MOST + min(PAIR_MOST - 1 - s, MOST - 1)]
-                for b in range(BLOCK // piece):
-                    at = pl.ds(b * piece, piece)
-                    for c, held in enumerate((kb[p], vb[p])):
+        for c, held in enumerate((kb[p], vb[p])):
+            arrived(c, p)
+            for d in range(1, S):
+                first = count_of(2 * p, tile_after(d), tile)
+                for s in range(PAIR_MOST):
+                    left = lsm[S - d - 1, 0, 2 * p * MOST + min(s, MOST - 1)]
+                    right = lsm[S - d - 1, 0, (2 * p + 1) * MOST + min(PAIR_MOST - 1 - s, MOST - 1)]
+                    for b in range(BLOCK // piece):
                         if s < PAIR_MOST - 1:
                             chosen = held[left * (BLOCK // piece) + b, :, :DH]
                         if s > 0:
@@ -176,8 +171,8 @@
                                 chosen = jnp.where(s < first, chosen, other)
                             else:
                                 chosen = other
-                        pk[p, d - 1, c, s, at, :] = chosen
-            z_copy(p, d).start()
+                        pk[p, d - 1, c, s, pl.ds(b * piece, piece), :] = chosen
+                z_copy(p, d, c).start()
 
     factor = math.log2(math.e) / math.sqrt(DH)
     width = MOST * BLOCK
@@ -185,7 +180,8 @@
     for p in range(pairs):
         arrived(2, p)
         for d in range(1, S):
-            z_copy(p, d).wait_recv()
+            for c in range(2):
+                z_copy(p, d, c).wait_recv()
 
         def chunk(i, carry, p=p):
             mine = row_range(peer_of(i))
@@ -230,7 +226,8 @@
     for d in range(1, S):
         l_copy(d).wait_send()
         for p in range(pairs):
-            z_copy(p, d).wait_send()
+            for c in range(2):
+                z_copy(p, d, c).wait_send()
     for p in range(pairs):
         for i in range(H - 1):
             for a in range(3):
@@ -269,8 +266,8 @@
             pltpu.SMEM((S - 1, 1, 128), jnp.int32),
             pltpu.SemaphoreType.DMA((3, pairs, H)),
             pltpu.SemaphoreType.DMA((3, pairs, H)),
-            pltpu.SemaphoreType.DMA((pairs, S - 1)),
-            pltpu.SemaphoreType.DMA((pairs, S - 1)),
+            pltpu.SemaphoreType.DMA((pairs, S - 1, 2)),
+            pltpu.SemaphoreType.DMA((pairs, S - 1, 2)),
             pltpu.SemaphoreType.DMA((S - 1,)),
             pltpu.SemaphoreType.DMA((S - 1,)),
             pltpu.SemaphoreType.DMA,

time: 119 us -> 116 us (0.975)
  the two profiles are of different devices: /device:TPU:8 before, /device:TPU:0 now
where the time goes in v2:
time: 116 us; the launch traced here: 115 us
  Pallas kernels  110 us (95%)
  local copies, waits for them, and re-layouts  5.75 us (5%)
    pallas_call x1, Pallas kernels, on_device(): pl.pallas_call(functools.partial(body, (H, S, rows, heads, piece)), out_s...  110 us
    unnamed x4, local copies, waits for them, and re-layouts  4.2 us

profile of v2, /device:TPU:0, one launch (start us, length us, event | category | flops | bytes accessed | tf_op | source)
XLA Modules:
  0.0 115.5 jit_solution(10868926435889684239)
XLA Ops:
  0.0 0.0 copy-start
  0.0 0.7 copy-done
  0.7 0.1 dynamic-slice_bitcast_fusion
  0.8 0.1 copy.8
  0.9 0.1 reshape.13
  0.9 0.6 pad.4.lists_ref
  1.5 0.8 copy.10
  2.3 0.7 reshape.14.counts_ref
  3.0 109.7 %block_attention.1 = bf16[192,4096]{1,0:T(8,128)(2,1)} custom-call(s32[4,1,128]{2,1,0:T(1,128)} %pad.4.lists_ref, s32[512]{0:T(512)} %reshape.14.counts_ref, bf16[192,4096]{1,0:T(8,128)(2,1)} %q_ref.1, bf16[3,64,4096]{2,1,0:T(8,128)(2,1)} %bitcast.7, bf16[3,64,4096]{2,1,0:T(8,128)(2,1)} %bitcast.8), custom_call_target="tpu_custom_call" | custom-call | tf_op jit(solution)/shard_map/block_attention/pallas_call | solution.py:255
  112.7 2.7 %copy.12 = bf16[192,4096]{1,0:T(8,128)(2,1)} copy(bf16[192,4096]{1,0:T(8,128)(2,1)} %block_attention.1) | data formatting | bytes 3145728
Async XLA Ops:
  0.0 0.7 copy-start

commit v3 on v2

--- a/solution.py
+++ b/solution.py
@@ -21,12 +21,12 @@
     return lax.dot_general(a, b, (((1,), (1,)), ((), ())), preferred_element_type=jnp.float32)
 
 
-def body(dims, lists_ref, counts_ref, q_ref, k_ref, v_ref, out_ref, *scratch):
+def body(dims, lists_ref, q_ref, k_ref, v_ref, out_ref, *scratch):
     H, S, rows, heads, piece = dims
     pairs = heads // 2
     chips = H // 2
     kb, vb, qb = scratch[:pairs], scratch[pairs : 2 * pairs], scratch[2 * pairs : 3 * pairs]
-    (ob, pk, fk, lbuf, lsm, x_send, x_recv, z_send, z_recv, l_send, l_recv, l_loc, o_send, o_recv) = (
+    (ob, pk, fk, lbuf, lsm, own_lists, x_send, x_recv, z_send, z_recv, l_send, l_recv, l_loc, o_send, o_recv) = (
         scratch[3 * pairs :]
     )
     me = lax.axis_index("head")
@@ -127,6 +127,8 @@
             ob.at[p, H - 1], out_ref.at[:, pair_columns(me, p)], o_recv.at[p, H - 1]
         )
 
+    own_scalars = pltpu.make_async_copy(lists_ref, own_lists, l_loc.at[1])
+    own_scalars.start()
     pl.semaphore_wait(barrier, H - 1 + S - 1)
     for d in range(1, S):
         l_copy(d).start()
@@ -142,7 +144,7 @@
 
     for d in range(1, S):
         l_copy(d).wait_recv()
-    to_scalars = pltpu.make_async_copy(lbuf, lsm, l_loc)
+    to_scalars = pltpu.make_async_copy(lbuf, lsm, l_loc.at[0])
     to_scalars.start()
     to_scalars.wait()
 
@@ -151,14 +153,16 @@
         for i in range(H - 1):
             x_copy(a, p, i, True).wait_recv()
 
+    own_scalars.wait()
+
     def count_of(head_slot, query_tile, key_tile):
-        return counts_ref[((me * heads + head_slot) * S + query_tile) * S + key_tile]
+        return own_lists[key_tile, 0, heads * MOST + head_slot]
 
     for p in range(pairs):
         for c, held in enumerate((kb[p], vb[p])):
             arrived(c, p)
             for d in range(1, S):
-                first = count_of(2 * p, tile_after(d), tile)
+                first = lsm[S - d - 1, 0, heads * MOST + 2 * p]
                 for s in range(PAIR_MOST):
                     left = lsm[S - d - 1, 0, 2 * p * MOST + min(s, MOST - 1)]
                     right = lsm[S - d - 1, 0, (2 * p + 1) * MOST + min(PAIR_MOST - 1 - s, MOST - 1)]
@@ -243,8 +247,13 @@
     heads = HEADS // H
     pairs = heads // 2
     mine = lax.dynamic_slice_in_dim(block_lists[:, 0], me * heads, heads)
-    lists = jnp.transpose(mine, (1, 0, 2)).reshape(S, 1, heads * MOST)
-    lists = jnp.pad(lists, ((0, 0), (0, 0), (0, 128 - heads * MOST)))
+    tile = lax.axis_index("seq")
+    counts = lax.dynamic_slice(block_counts, (me * heads, tile, 0), (heads, 1, S))
+    lists = jnp.concatenate(
+        [jnp.transpose(mine, (1, 0, 2)).reshape(S, heads * MOST), jnp.transpose(counts[:, 0])],
+        axis=1,
+    )
+    lists = jnp.pad(lists, ((0, 0), (0, 128 - heads * (MOST + 1))))[:, None]
     bf16 = jnp.bfloat16
     piece = math.gcd(rows, BLOCK)
     pieces = (rows // piece, piece, query_rows.shape[1])
@@ -255,7 +264,7 @@
     return pl.pallas_call(
         functools.partial(body, (H, S, rows, heads, piece)),
         out_shape=jax.ShapeDtypeStruct(query_rows.shape, bf16),
-        in_specs=[anywhere, pl.BlockSpec(memory_space=pltpu.SMEM), anywhere, anywhere, anywhere],
+        in_specs=[anywhere] * 4,
         out_specs=anywhere,
         scratch_shapes=tile_buffers
         + [
@@ -264,13 +273,14 @@
             pltpu.VMEM((pairs, S - 1, 2, PAIR_MOST, BLOCK, DH), bf16),
             pltpu.VMEM((S - 1, 1, 128), jnp.int32),
             pltpu.SMEM((S - 1, 1, 128), jnp.int32),
+            pltpu.SMEM((S, 1, 128), jnp.int32),
             pltpu.SemaphoreType.DMA((3, pairs, H)),
             pltpu.SemaphoreType.DMA((3, pairs, H)),
             pltpu.SemaphoreType.DMA((pairs, S - 1, 2)),
             pltpu.SemaphoreType.DMA((pairs, S - 1, 2)),
             pltpu.SemaphoreType.DMA((S - 1,)),
             pltpu.SemaphoreType.DMA((S - 1,)),
-            pltpu.SemaphoreType.DMA,
+            pltpu.SemaphoreType.DMA((2,)),
             pltpu.SemaphoreType.DMA((pairs, H)),
             pltpu.SemaphoreType.DMA((pairs, H)),
         ],
@@ -278,7 +288,7 @@
             collective_id=0, has_side_effects=True, vmem_limit_bytes=60 << 20
         ),
         name="block_attention",
-    )(lists, block_counts.reshape(-1), query_rows, key_rows.reshape(pieces), value_rows.reshape(pieces))
+    )(lists, query_rows, key_rows.reshape(pieces), value_rows.reshape(pieces))
 
 
 def solution(mesh):

time: 116 us -> 114 us (0.983)
    unnamed x4 -> x3, local copies, waits for them, and re-layouts: 4.2 us -> 3.4 us
where the time goes in v3:
time: 114 us
  Pallas kernels  109 us (96%)
  local copies, waits for them, and re-layouts  5.01 us (4%)
    pallas_call x1, Pallas kernels, on_device(): pl.pallas_call(functools.partial(body, (H, S, rows, heads, piece)), out_s...  109 us
    unnamed x3, local copies, waits for them, and re-layouts  3.4 us

profile of v3, /device:TPU:0, one launch (start us, length us, event | category | flops | bytes accessed | tf_op | source)
XLA Modules:
  0.0 114.1 jit_solution(15976443026410225614)
XLA Ops:
  0.0 0.0 copy-start
  0.0 0.7 copy-done
  0.7 0.1 dynamic-slice_bitcast_fusion.1
  0.8 0.8 dynamic-slice_bitcast_fusion
  1.5 0.1 copy.7
  1.6 0.1 reshape.10
  1.7 0.1 pad_add_fusion
  1.8 0.6 pad.4
  2.4 109.0 %block_attention.1 = bf16[192,4096]{1,0:T(8,128)(2,1)} custom-call(s32[4,1,128]{2,1,0:T(1,128)} %bitcast.13, bf16[192,4096]{1,0:T(8,128)(2,1)} %q_ref.1, bf16[3,64,4096]{2,1,0:T(8,128)(2,1)} %bitcast.11, bf16[3,64,4096]{2,1,0:T(8,128)(2,1)} %bitcast.12), custom_call_target="tpu_custom_call" | custom-call | tf_op jit(solution)/shard_map/block_attention/pallas_call | solution.py:264
  111.4 2.7 %copy.9 = bf16[192,4096]{1,0:T(8,128)(2,1)} copy(bf16[192,4096]{1,0:T(8,128)(2,1)} %block_attention.1) | data formatting | bytes 3145728
Async XLA Ops:
  0.0 0.7 copy-start
